TPU v7x, 32 devices: a whole 2x2x4 slice. The times are simulated.
32 devices in a mesh: quad: 2 (over x), py: 4 (over y, core), pz: 4 (over z).
Axes of the slice: x: 2, y: 2, z: 4, core: 2. Of those that a mesh axis runs over, the one named last changes fastest.
Arguments:
- source_real: float32 [4, 16, 64, 512], P(None, None, 'py', 'pz'), may hold values from -6 to 6
- source_imag: float32 [4, 16, 64, 512], P(None, None, 'py', 'pz'), may hold values from -2 to 2
- potential: float32 [16, 64, 512], P(None, 'py', 'pz'), may hold values from 0 to 2
- center: float32 [1], replicated, may hold values from 4.5 to 6
- radius: float32 [1], replicated, may hold values from 1 to 2
Outputs:
- moments: float32 [4, 2, 4, 16, 64, 512], P(None, None, None, 'quad', 'py', 'pz')
All inputs are finite; a program needn't handle non-finite values.
Results may differ from a plain program's by a relative error of at most 0.0003.
Values sent between devices are 32-bit elements; how exact they have to be, the bound alone decides.
No kernel may reach another device: no remote copies, remote signals or barrier semaphores. Data moves between devices by JAX's collectives and lax.ppermute only.
A program may use at most 256 MiB of HBM per device.

v0:
```python
import math
import jax
import jax.numpy as jnp
from jax import lax
from jax.sharding import PartitionSpec as P

QPTS = 8
MOMS = 4
stencil_weights = (-205.0 / 72.0, 8.0 / 5.0, -1.0 / 5.0, 8.0 / 315.0, -1.0 / 560.0)


def padded_2(block, sides, width):
    for axis, dim in sides:
        count = lax.axis_size(axis)
        forward = [(i, i + 1) for i in range(count - 1)]
        forward.append((count - 1, 0))
        backward = [(target, source) for source, target in forward]
        low = lax.ppermute(
            lax.slice_in_dim(block, block.shape[dim] - width, None, axis=dim), axis, forward
        )
        high = lax.ppermute(lax.slice_in_dim(block, 0, width, axis=dim), axis, backward)
        block = jnp.concatenate([low, block, high], axis=dim)
    return block


def apply_operator(field, potential):
    padded = padded_2(field, (("py", 4), ("pz", 5)), 4)
    width_y = field.shape[4]
    width_z = field.shape[5]
    laplace = 3.0 * stencil_weights[0] * field
    for offset in range(1, 5):
        beside_all = jnp.roll(field, offset, 3) + jnp.roll(field, -offset, 3)
        beside_all = (
            beside_all + padded[:, :, :, :, 4 + offset : 4 + offset + width_y, 4 : 4 + width_z]
        )
        beside_all = (
            beside_all + padded[:, :, :, :, 4 - offset : 4 - offset + width_y, 4 : 4 + width_z]
        )
        beside_all = (
            beside_all + padded[:, :, :, :, 4 : 4 + width_y, 4 + offset : 4 + offset + width_z]
        )
        beside_all = (
            beside_all + padded[:, :, :, :, 4 : 4 + width_y, 4 - offset : 4 - offset + width_z]
        )
        laplace = laplace + stencil_weights[offset] * beside_all
    return -0.5 * laplace + potential * field


def complex_mul(left, right):
    return (left[0] * right[0] - left[1] * right[1], left[0] * right[1] + left[1] * right[0])


def complex_div(left, right):
    norm_sq = right[0] * right[0] + right[1] * right[1]
    return (
        (left[0] * right[0] + left[1] * right[1]) / norm_sq,
        (left[1] * right[0] - left[0] * right[1]) / norm_sq,
    )


def local_bilinear(left, right):
    both = complex_mul(left, right)
    return (jnp.sum(both[0], axis=(-3, -2, -1)), jnp.sum(both[1], axis=(-3, -2, -1)))


def spread(value):
    return (value[0][..., None, None, None], value[1][..., None, None, None])


def moment_terms(solution, angles, radius_value):
    orders = jnp.arange(1, MOMS + 1).astype(jnp.float32)
    phase = orders[:, None] * angles[None, :]
    weight_re = radius_value / QPTS * jnp.cos(phase)
    weight_im = radius_value / QPTS * jnp.sin(phase)
    highest = lax.Precision.HIGHEST
    real_part = jnp.einsum("kq,qsxyz->ksxyz", weight_re, solution[:, 0], precision=highest)
    real_part = real_part - jnp.einsum(
        "kq,qsxyz->ksxyz", weight_im, solution[:, 1], precision=highest
    )
    imag_part = jnp.einsum("kq,qsxyz->ksxyz", weight_re, solution[:, 1], precision=highest)
    imag_part = imag_part + jnp.einsum(
        "kq,qsxyz->ksxyz", weight_im, solution[:, 0], precision=highest
    )
    return jnp.stack([real_part, imag_part], 1)


def per_device(source_real, source_imag, potential, center, radius):
    groups = lax.axis_size("quad")
    local_count = QPTS // groups
    first_point = lax.axis_index("quad") * local_count
    indices = (first_point + jnp.arange(local_count)).astype(jnp.float32)
    angles = 2.0 * math.pi * (indices + 0.5) / QPTS
    shift_re = center[0] + radius[0] * jnp.cos(angles)
    shift_im = radius[0] * jnp.sin(angles)
    shift_pair = (shift_re[:, None], shift_im[:, None])
    shift_field = (shift_re[:, None, None, None, None], shift_im[:, None, None, None, None])
    source = (source_real, source_imag)
    applied = apply_operator(jnp.stack(source)[None], potential)[0]
    hsource = (applied[0], applied[1])
    rho_local = local_bilinear(source, source)
    curv_local = local_bilinear(source, hsource)
    totals = lax.psum((rho_local[0], rho_local[1], curv_local[0], curv_local[1]), ("py", "pz"))
    rho_first = (totals[0], totals[1])
    curv_first = (totals[2], totals[3])
    scaled = complex_mul(shift_pair, rho_first)
    denom = (scaled[0] - curv_first[0], scaled[1] - curv_first[1])
    alpha_first = complex_div(rho_first, denom)
    alpha_wide = spread(alpha_first)
    first_iterate = complex_mul(alpha_wide, source)
    shifted = complex_mul(shift_field, source)
    image = (shifted[0] - hsource[0], shifted[1] - hsource[1])
    moved = complex_mul(alpha_wide, image)
    residual = (source[0] - moved[0], source[1] - moved[1])
    hres = apply_operator(jnp.stack(residual, 1), potential)
    shifted_res = complex_mul(shift_field, residual)
    image_res = (shifted_res[0] - hres[:, 0], shifted_res[1] - hres[:, 1])
    rho_part = local_bilinear(residual, residual)
    mixed_part = local_bilinear(residual, image_res)
    paired = lax.psum((rho_part[0], rho_part[1], mixed_part[0], mixed_part[1]), ("py", "pz"))
    rho_next = (paired[0], paired[1])
    mixed = (paired[2], paired[3])
    beta = complex_div(rho_next, rho_first)
    carried = complex_mul(spread(beta), source)
    direction = (residual[0] + carried[0], residual[1] + carried[1])
    correction = complex_div(complex_mul(beta, rho_next), alpha_first)
    curv_next = (mixed[0] - correction[0], mixed[1] - correction[1])
    alpha_next = complex_div(rho_next, curv_next)
    step_part = complex_mul(spread(alpha_next), direction)
    solution = jnp.stack((first_iterate[0] + step_part[0], first_iterate[1] + step_part[1]), 1)
    terms = moment_terms(solution, angles, radius[0])
    return lax.psum_scatter(terms, "quad", scatter_dimension=3, tiled=True)


def solution(mesh):
    in_specs = (P(None, None, "py", "pz"), P(None, None, "py", "pz"), P(None, "py", "pz"), P(), P())
    out_specs = P(None, None, None, "quad", "py", "pz")
    return jax.shard_map(
        per_device, mesh=mesh, in_specs=in_specs, out_specs=out_specs, check_vma=False
    )
```

profile of v0, /device:TPU:0, one launch (start us, length us, event | category | flops | bytes accessed | tf_op | source)
XLA Modules:
  0.0 492.0 jit_solution(7060185690487794828)
XLA Ops:
  51.3 4.5 fusion.50
  63.6 17.7 %fusion.58 = f32[1,2,4,16,16,128]{5,4,3,2,1,0:T(8,128)S(1)} fusion(f32[1,2,4,16,24,4]{5,4,3,2,1,0:T(8,128)} %copy.96, f32[1,2,4,16,24,128]{5,4,3,2,1,0:T(8,128)} %copy.93, f32[1,2,4,16,24,4]{5,4,3,2,1,0:T(8,128)} %copy.94, f32[1,2,4,15,16,128]{5,4,3,2,1,0:T(8,128)} %copy.87, f32[1,2,4,1,16,128]{5,4,3,2,1,0:T(8,128)} %bitcast.76, ...), kind=kLoop, calls=%fused_computation.166 | loop fusion | flops 12845056 | bytes 20676608 | tf_op jit(solution)/shard_map/add | solution.py:46
  82.9 34.7 %all-reduce.1 = (f32[4]{0:T(128)S(1)}, f32[4]{0:T(128)S(1)}, f32[4]{0:T(128)S(1)}, f32[4]{0:T(128)S(1)}) all-reduce(f32[4]{0:T(128)S(1)} %get-tuple-element.10, f32[4]{0:T(128)S(1)} %get-tuple-element.9, f32[4]{0:T(128)S(1)} %get-tuple-element.12, f32[4]{0:T(128)S(1)} %get-tuple-element.11), channel_id=1, replica_groups=mesh['quad'=2,'py'=4,'pz'=4] {'py','pz'}, use_global_device_ids=true, to_apply=%region_7.8 | all-reduce | flops 16 | bytes 128 | tf_op jit(solution)/shard_map/psum | solution.py:102
  124.4 3.5 fusion.31
  133.6 19.1 %copy.121 = f32[4,2,4,16,16,128]{4,3,5,2,1,0:T(8,128)} copy(f32[4,2,4,16,16,128]{5,4,3,2,1,0:T(8,128)} %pad_maximum_fusion.1) | data formatting | bytes 8388608 | tf_op jit(solution)/shard_map/stack | solution.py:114
  155.3 3.4 fusion.29
  161.9 3.4 fusion.25
  165.4 18.9 %copy.122 = f32[4,2,4,16,4,128]{4,3,5,2,1,0:T(8,128)} copy(f32[4,2,4,16,4,128]{5,3,4,2,1,0:T(8,128)} %collective-permute-done.4) | data formatting | bytes 2097152 | tf_op jit(solution)/shard_map/ppermute | solution.py:21
  184.3 18.6 %copy.120 = f32[4,2,4,16,4,128]{4,3,5,2,1,0:T(8,128)} copy(f32[4,2,4,16,4,128]{5,3,4,2,1,0:T(8,128)} %collective-permute-done.5) | data formatting | bytes 2097152 | tf_op jit(solution)/shard_map/ppermute | solution.py:18
  202.9 43.9 %pad_maximum_fusion = f32[4,2,4,16,24,128]{4,3,5,2,1,0:T(8,128)} fusion(f32[4,2,4,16,4,128]{4,3,5,2,1,0:T(8,128)} %copy.122, f32[4,2,4,16,16,128]{4,3,5,2,1,0:T(8,128)} %copy.121, f32[4,2,4,16,4,128]{4,3,5,2,1,0:T(8,128)} %copy.120), kind=kLoop, calls=%fused_computation | loop fusion | flops 3145728 | bytes 12582912 | tf_op jit(solution)/shard_map/concatenate | solution.py:22
  249.9 4.0 collective-permute-start.6
  257.3 5.5 %pad_maximum_fusion.2 = (f32[4,2,4,16,20,128]{5,4,3,2,1,0:T(8,128)}, f32[4,2,4,16,20,128]{5,4,3,2,1,0:T(8,128)}) fusion(f32[4,2,4,16,4,128]{5,4,3,2,1,0:T(4,128)S(1)} %copy.117, f32[4,1,4,16,16,128]{5,4,3,2,1,0:T(8,128)S(1)} %get-tuple-element.48, f32[4,1,4,16,16,128]{5,4,3,2,1,0:T(8,128)S(1)} %copy-done.2, f32[4,2,4,16,4,128]{5,4,3,2,1,0:T(4,128)S(1)} %copy.119), kind=kLoop, calls=%fused_computation.50 | loop fusion | flops 5242880 | bytes 16777216 | tf_op jit(solution)/shard_map/concatenate | solution.py:22
  262.7 22.1 %copy.123 = f32[4,2,4,16,24,128]{5,4,3,2,1,0:T(8,128)} copy(f32[4,2,4,16,24,128]{4,3,5,2,1,0:T(8,128)} %pad_maximum_fusion) | data formatting | bytes 12582912 | tf_op jit(solution)/shard_map/concatenate | solution.py:22
  284.8 6.1 %copy.125 = f32[4,2,4,16,24,4]{5,4,3,2,1,0:T(8,128)} copy(f32[4,2,4,16,24,4]{4,3,5,2,1,0:T(8,128)} %collective-permute-done.7) | data formatting | bytes 393216 | tf_op jit(solution)/shard_map/ppermute | solution.py:18
  291.0 7.0 %collective-permute-done.6 = f32[4,2,4,16,24,4]{4,3,5,2,1,0:T(8,128)} collective-permute-done((f32[4,2,4,16,24,4]{4,3,5,2,1,0:T(8,128)}, f32[4,2,4,16,24,4]{4,3,5,2,1,0:T(8,128)}, u32[]{:S(2)}, u32[]{:S(2)}) %collective-permute-start.6) | collective-permute-done | bytes 196640 | tf_op jit(solution)/shard_map/ppermute | solution.py:21
  298.0 6.0 %copy.124 = f32[4,2,4,16,24,4]{5,4,3,2,1,0:T(8,128)} copy(f32[4,2,4,16,24,4]{4,3,5,2,1,0:T(8,128)} %collective-permute-done.6) | data formatting | bytes 393216 | tf_op jit(solution)/shard_map/ppermute | solution.py:21
  304.0 62.2 %fusion.6 = f32[4,2,4,16,16,128]{5,4,3,2,1,0:T(8,128)} fusion(f32[4,2,4,16,24,4]{5,4,3,2,1,0:T(8,128)} %copy.125, f32[4,2,4,16,24,128]{5,4,3,2,1,0:T(8,128)} %copy.123, f32[4,2,4,16,24,4]{5,4,3,2,1,0:T(8,128)} %copy.124, f32[4,2,4,16,20,128]{5,4,3,2,1,0:T(8,128)} %get-tuple-element.43, f32[4,2,4,16,20,128]{5,4,3,2,1,0:T(8,128)} %get-tuple-element.42, ...), kind=kLoop, calls=%fused_computation.70 | loop fusion | flops 51380224 | bytes 82313216 | tf_op jit(solution)/shard_map/add | solution.py:46
  366.3 5.0 %subtract_reduce_fusion = (f32[4,4]{1,0:T(4,128)S(1)}, f32[4,4]{1,0:T(4,128)S(1)}, f32[4,4]{1,0:T(4,128)S(1)}, f32[4,4]{1,0:T(4,128)S(1)}) fusion(f32[4,2,4,16,16,128]{5,4,3,2,1,0:T(8,128)} %fusion.6, f32[4]{0:T(128)S(1)} %get-tuple-element.88, f32[4]{0:T(128)S(1)} %get-tuple-element.89, f32[4,16,16,128]{3,2,1,0:T(8,128)S(1)} %copy-done.8, ...), kind=kLoop, calls=%fused_computation.129 | loop fusion | flops 20447168 | bytes 6291872 | tf_op jit(solution)/shard_map/reduce_sum | solution.py:63
  371.3 30.6 %all-reduce = (f32[4,4]{1,0:T(4,128)S(1)}, f32[4,4]{1,0:T(4,128)S(1)}, f32[4,4]{1,0:T(4,128)S(1)}, f32[4,4]{1,0:T(4,128)S(1)}) all-reduce(f32[4,4]{1,0:T(4,128)S(1)} %get-tuple-element.8, f32[4,4]{1,0:T(4,128)S(1)} %get-tuple-element.6, f32[4,4]{1,0:T(4,128)S(1)} %get-tuple-element.7, ...), channel_id=1, replica_groups=mesh['quad'=2,'py'=4,'pz'=4] {'py','pz'}, use_global_device_ids=true, to_apply=%region_9.10 | all-reduce | flops 64 | bytes 512 | tf_op jit(solution)/shard_map/psum | solution.py:119
  405.1 4.4 fusion.34
  409.5 4.4 fusion.36
  413.9 4.6 add_bitcast_fusion
  418.5 4.9 %subtract_bitcast_fusion = f32[4,1,4,16,16,128]{5,0,4,3,2,1:T(4,128)S(1)} fusion(f32[4,4,16,16,128]{4,0,3,2,1:T(4,128)S(1)} %fusion.36, f32[4,4,16,16,128]{4,3,2,1,0:T(8,128)S(1)} %get-tuple-element.46, f32[4]{0:T(128)S(1)} %copy-done.20, f32[4]{0:T(128)S(1)} %copy-done.21, f32[]{:T(128)S(6)} %div.49), kind=kOutput, calls=%fused_computation.123 | convolution fusion | flops 25690144 | bytes 6291492 | tf_op jit(solution)/shard_map/kq,qsxyz->ksxyz/dot_general | solution.py:76
  428.1 53.6 %reduce-scatter.2.cloned.1.call-done = f32[4,2,4,8,16,128]{5,4,2,1,0,3:T(8,128)} async-done(((f32[4,2,4,16,16,128]{5,4,2,1,0,3:T(8,128)}), f32[4,2,4,8,16,128]{5,4,2,1,0,3:T(8,128)}) %reduce-scatter.2.cloned.1.call-update) | async-done | bytes 2097168 | tf_op jit(solution)/shard_map/reduce_scatter | solution.py:131
  (136 shorter events, 88.3 us)
Async XLA Ops:
  6.5 475.1 %reduce-scatter.2.cloned.1.call-start = ((), (), s32[]{:S(2)}) async-start(), calls=%async_computation.1 | async-start | bytes 6291456 | tf_op jit(solution)/shard_map/reduce_scatter | solution.py:131
  9.0 28.6 %collective-permute-start = (f32[1,2,4,16,4,128]{5,3,4,2,1,0:T(8,128)}, f32[1,2,4,16,4,128]{5,3,4,2,1,0:T(8,128)}, u32[]{:S(2)}, u32[]{:S(2)}) collective-permute-start(f32[1,2,4,16,4,128]{5,3,4,2,1,0:T(8,128)} %get-tuple-element.83), channel_id=1, source_target_pairs={{4,0},{8,4},{12,8},{0,12},{5,1},{9,5},{13,9},{1,13},{6,2},{10,6},{... | collective-permute-start | bytes 786440 | tf_op jit(solution)/shard_map/ppermute | solution.py:21
  11.4 26.2 %collective-permute-start.1 = (f32[1,2,4,16,4,128]{5,3,4,2,1,0:T(8,128)}, f32[1,2,4,16,4,128]{5,3,4,2,1,0:T(8,128)}, u32[]{:S(2)}, u32[]{:S(2)}) collective-permute-start(f32[1,2,4,16,4,128]{5,3,4,2,1,0:T(8,128)} %get-tuple-element.82), channel_id=1, source_target_pairs={{0,4},{4,8},{8,12},{12,0},{1,5},{5,9},{9,13},{13,1},{2,6},{6,10},{... | collective-permute-start | bytes 786440 | tf_op jit(solution)/shard_map/ppermute | solution.py:18
  44.0 13.5 %collective-permute-start.3 = (f32[1,2,4,16,24,4]{4,3,5,2,1,0:T(8,128)}, f32[1,2,4,16,24,4]{4,3,5,2,1,0:T(8,128)}, u32[]{:S(2)}, u32[]{:S(2)}) collective-permute-start(f32[1,2,4,16,24,4]{4,3,5,2,1,0:T(8,128)} %copy.95), channel_id=1, source_target_pairs={{0,1},{1,2},{2,3},{3,0},{4,5},{5,6},{6,7},{7,4},{8,9},{9,10},{10,1... | collective-permute-start | bytes 147464 | tf_op jit(solution)/shard_map/ppermute | solution.py:18
  48.5 12.1 %collective-permute-start.2 = (f32[1,2,4,16,24,4]{4,3,5,2,1,0:T(8,128)}, f32[1,2,4,16,24,4]{4,3,5,2,1,0:T(8,128)}, u32[]{:S(2)}, u32[]{:S(2)}) collective-permute-start(f32[1,2,4,16,24,4]{4,3,5,2,1,0:T(8,128)} %copy.92), channel_id=1, source_target_pairs={{1,0},{2,1},{3,2},{0,3},{5,4},{6,5},{7,6},{4,7},{9,8},{10,9},{11,1... | collective-permute-start | bytes 147464 | tf_op jit(solution)/shard_map/ppermute | solution.py:21
  55.8 7.8 %copy-start.3 = (f32[4,16,16,128]{3,2,1,0:T(8,128)S(1)}, f32[4,16,16,128]{3,2,1,0:T(8,128)}, u32[]{:S(2)}) copy-start(f32[4,16,16,128]{3,2,1,0:T(8,128)} %param.6) | copy-start | bytes 1572868
  55.8 7.8 %copy-start.4 = (f32[4,16,16,128]{3,2,1,0:T(8,128)S(1)}, f32[4,16,16,128]{3,2,1,0:T(8,128)}, u32[]{:S(2)}) copy-start(f32[4,16,16,128]{3,2,1,0:T(8,128)} %param.5) | copy-start | bytes 1572868
  81.3 36.4 %copy-start.5 = (f32[4,16,16,128]{3,2,1,0:T(8,128)S(1)}, f32[4,16,16,128]{3,2,1,0:T(8,128)}, u32[]{:S(2)}) copy-start(f32[4,16,16,128]{3,2,1,0:T(8,128)} %param.5) | copy-start | bytes 1572868
  117.6 11.8 %copy-start.26 = (f32[4]{0:T(128)}, f32[4]{0:T(128)S(1)}, u32[]{:S(2)}) copy-start(f32[4]{0:T(128)S(1)} %get-tuple-element.19) | copy-start | bytes 52
  117.6 11.8 %copy-start.28 = (f32[4]{0:T(128)}, f32[4]{0:T(128)S(1)}, u32[]{:S(2)}) copy-start(f32[4]{0:T(128)S(1)} %get-tuple-element.20) | copy-start | bytes 52
  120.2 12.7 %copy-start = (f32[4,1,4,16,16,128]{5,4,3,2,1,0:T(8,128)}, f32[4,1,4,16,16,128]{5,4,3,2,1,0:T(8,128)S(1)}, u32[]{:S(2)}) copy-start(f32[4,1,4,16,16,128]{5,4,3,2,1,0:T(8,128)S(1)} %get-tuple-element.49) | copy-start | bytes 6291460
  131.1 34.3 %collective-permute-start.4 = (f32[4,2,4,16,4,128]{5,3,4,2,1,0:T(8,128)}, f32[4,2,4,16,4,128]{5,3,4,2,1,0:T(8,128)}, u32[]{:S(2)}, u32[]{:S(2)}) collective-permute-start(f32[4,2,4,16,4,128]{5,3,4,2,1,0:T(8,128)} %copy.144), channel_id=1, source_target_pairs={{4,0},{8,4},{12,8},{0,12},{5,1},{9,5},{13,9},{1,13},{6,2},{10,6},{... | collective-permute-start | bytes 3145736 | tf_op jit(solution)/shard_map/ppermute | solution.py:21
  132.2 52.1 %collective-permute-start.5 = (f32[4,2,4,16,4,128]{5,3,4,2,1,0:T(8,128)}, f32[4,2,4,16,4,128]{5,3,4,2,1,0:T(8,128)}, u32[]{:S(2)}, u32[]{:S(2)}) collective-permute-start(f32[4,2,4,16,4,128]{5,3,4,2,1,0:T(8,128)} %copy.145), channel_id=1, source_target_pairs={{0,4},{4,8},{8,12},{12,0},{1,5},{5,9},{9,13},{13,1},{2,6},{6,10},{... | collective-permute-start | bytes 3145736 | tf_op jit(solution)/shard_map/ppermute | solution.py:18
  249.9 34.9 %collective-permute-start.7 = (f32[4,2,4,16,24,4]{4,3,5,2,1,0:T(8,128)}, f32[4,2,4,16,24,4]{4,3,5,2,1,0:T(8,128)}, u32[]{:S(2)}, u32[]{:S(2)}) collective-permute-start(f32[4,2,4,16,24,4]{4,3,5,2,1,0:T(8,128)} %get-tuple-element.25), channel_id=1, source_target_pairs={{0,1},{1,2},{2,3},{3,0},{4,5},{5,6},{6,7},{7,4},{8,9},{9,10},{10,1... | collective-permute-start | bytes 589832 | tf_op jit(solution)/shard_map/ppermute | solution.py:18
  249.9 48.1 %collective-permute-start.6 = (f32[4,2,4,16,24,4]{4,3,5,2,1,0:T(8,128)}, f32[4,2,4,16,24,4]{4,3,5,2,1,0:T(8,128)}, u32[]{:S(2)}, u32[]{:S(2)}) collective-permute-start(f32[4,2,4,16,24,4]{4,3,5,2,1,0:T(8,128)} %get-tuple-element.24), channel_id=1, source_target_pairs={{1,0},{2,1},{3,2},{0,3},{5,4},{6,5},{7,6},{4,7},{9,8},{10,9},{11,1... | collective-permute-start | bytes 589832 | tf_op jit(solution)/shard_map/ppermute | solution.py:21
  304.0 62.2 %copy-start.6 = (f32[4,16,16,128]{3,2,1,0:T(8,128)S(1)}, f32[4,16,16,128]{3,2,1,0:T(8,128)}, u32[]{:S(2)}) copy-start(f32[4,16,16,128]{3,2,1,0:T(8,128)} %get-tuple-element.60) | copy-start | bytes 1572868
  304.0 62.2 %copy-start.8 = (f32[4,16,16,128]{3,2,1,0:T(8,128)S(1)}, f32[4,16,16,128]{3,2,1,0:T(8,128)}, u32[]{:S(2)}) copy-start(f32[4,16,16,128]{3,2,1,0:T(8,128)} %get-tuple-element.61) | copy-start | bytes 1572868
  366.3 35.7 %copy-start.23 = (f32[4]{0:T(128)S(1)}, f32[4]{0:T(128)}, u32[]{:S(2)}) copy-start(f32[4]{0:T(128)} %copy-done.22) | copy-start | bytes 52
  366.3 35.7 %copy-start.25 = (f32[4]{0:T(128)S(1)}, f32[4]{0:T(128)}, u32[]{:S(2)}) copy-start(f32[4]{0:T(128)} %copy-done.24) | copy-start | bytes 52
  366.3 35.7 %copy-start.27 = (f32[4]{0:T(128)S(1)}, f32[4]{0:T(128)}, u32[]{:S(2)}) copy-start(f32[4]{0:T(128)} %copy-done.26) | copy-start | bytes 52
  366.3 35.7 %copy-start.29 = (f32[4]{0:T(128)S(1)}, f32[4]{0:T(128)}, u32[]{:S(2)}) copy-start(f32[4]{0:T(128)} %copy-done.28) | copy-start | bytes 52
  366.3 35.7 %copy-start.30 = (f32[4]{0:T(128)S(1)}, f32[4]{0:T(128)}, u32[]{:S(2)}) copy-start(f32[4]{0:T(128)} %multiply_add_fusion.4) | copy-start | bytes 52
  366.3 35.8 %copy-start.7 = (f32[4,16,16,128]{3,2,1,0:T(8,128)S(1)}, f32[4,16,16,128]{3,2,1,0:T(8,128)}, u32[]{:S(2)}) copy-start(f32[4,16,16,128]{3,2,1,0:T(8,128)} %get-tuple-element.60) | copy-start | bytes 1572868
  366.3 35.8 %copy-start.9 = (f32[4,16,16,128]{3,2,1,0:T(8,128)S(1)}, f32[4,16,16,128]{3,2,1,0:T(8,128)}, u32[]{:S(2)}) copy-start(f32[4,16,16,128]{3,2,1,0:T(8,128)} %get-tuple-element.61) | copy-start | bytes 1572868
  (16 other events, 82.4 us)
Sparse Core Ops, SparseCore 0:
  428.2 53.3 reduce-scatter.1
where the time goes:
time: 499 us; the launch traced here: 492 us
  other arithmetic  173 us (35%)
  local copies, waits for them, and re-layouts  147 us (29%)
  blocking collectives  65.3 us (13%)
  waiting for transfers between devices  60.8 us (12%)
  matrix products  18.3 us (4%)
  between operations  15.5 us (3%)
  starting transfers between devices  11.4 us (2%)
    add x2, other arithmetic, apply_operator(): return -0.5 * laplace + potential * field  79.9 us
    concatenate x4, other arithmetic, padded_2(): block = jnp.concatenate([low, block, high], axis=dim)  55 us
    reduce_scatter x1, waiting for transfers between devices, per_device(): return lax.psum_scatter(terms, 'quad', scatter_dimension=3, tiled=True)  53.6 us
    psum x1, blocking collectives, per_device(): lax.psum((rho_local[0], rho_local[1], curv_local[0], curv_local[1]), ('py...  34.7 us
    psum x1, blocking collectives, per_device(): lax.psum((rho_part[0], rho_part[1], mixed_part[0], mixed_part[1]), ('py',...  30.6 us
    ppermute x4, local copies, waits for them, and re-layouts, padded_2(): lax.ppermute(lax.slice_in_dim(block, 0, width, axis=dim), axis, backward)  29.5 us
    ppermute x4, local copies, waits for them, and re-layouts, padded_2(): lax.ppermute(lax.slice_in_dim(block, block.shape[dim] - width, None, axis...  29.4 us
    concatenate x2, local copies, waits for them, and re-layouts, padded_2(): block = jnp.concatenate([low, block, high], axis=dim)  23.7 us
  transfers between devices with their start and end apart: 9, of which 3 were waited for; matrix products, arithmetic and copies ran while one was open for 26% of the time, Pallas kernels for 0%

commit v1 on v0

--- a/solution.py
+++ b/solution.py
@@ -7,6 +7,11 @@
 QPTS = 8
 MOMS = 4
 stencil_weights = (-205.0 / 72.0, 8.0 / 5.0, -1.0 / 5.0, 8.0 / 315.0, -1.0 / 560.0)
+
+
+def axis_by_axis(array, inner_axis, outer_axis):
+    inner = lax.psum(array, inner_axis)
+    return lax.psum(inner, outer_axis)
 
 
 def padded_2(block, sides, width):
@@ -99,7 +104,7 @@
     hsource = (applied[0], applied[1])
     rho_local = local_bilinear(source, source)
     curv_local = local_bilinear(source, hsource)
-    totals = lax.psum((rho_local[0], rho_local[1], curv_local[0], curv_local[1]), ("py", "pz"))
+    totals = axis_by_axis((rho_local[0], rho_local[1], curv_local[0], curv_local[1]), "py", "pz")
     rho_first = (totals[0], totals[1])
     curv_first = (totals[2], totals[3])
     scaled = complex_mul(shift_pair, rho_first)

time: 499 us -> 485 us (0.972)
  blocking collectives: 65.3 us -> 52 us
    psum x1 -> x2, blocking collectives: 34.7 us -> 19.6 us  [the longest x1 12.9 us: axis_by_axis(): return lax.psum(inner, outer_axis)]
where the time goes in v1:
time: 485 us; the launch traced here: 478 us
  other arithmetic  174 us (36%)
  local copies, waits for them, and re-layouts  147 us (30%)
  waiting for transfers between devices  59.6 us (12%)
  blocking collectives  52 us (11%)
  matrix products  18.3 us (4%)
  between operations  15.5 us (3%)
  starting transfers between devices  11.4 us (2%)
    add x2, other arithmetic, apply_operator(): return -0.5 * laplace + potential * field  80.9 us
    concatenate x4, other arithmetic, padded_2(): block = jnp.concatenate([low, block, high], axis=dim)  54.9 us
    reduce_scatter x1, waiting for transfers between devices, per_device(): return lax.psum_scatter(terms, 'quad', scatter_dimension=3, tiled=True)  52.3 us
    psum x1, blocking collectives, per_device(): lax.psum((rho_part[0], rho_part[1], mixed_part[0], mixed_part[1]), ('py',...  32.4 us
    ppermute x4, local copies, waits for them, and re-layouts, padded_2(): lax.ppermute(lax.slice_in_dim(block, 0, width, axis=dim), axis, backward)  29.5 us
    ppermute x4, local copies, waits for them, and re-layouts, padded_2(): lax.ppermute(lax.slice_in_dim(block, block.shape[dim] - width, None, axis...  29.4 us
    concatenate x2, local copies, waits for them, and re-layouts, padded_2(): block = jnp.concatenate([low, block, high], axis=dim)  23.7 us
    slice x22, local copies, waits for them, and re-layouts, apply_operator(): beside_all = jnp.roll(field, offset, 3) + jnp.roll(field, -offset, 3)  23.7 us
  transfers between devices with their start and end apart: 9, of which 3 were waited for; matrix products, arithmetic and copies ran while one was open for 26% of the time, Pallas kernels for 0%

profile of v1, /device:TPU:0, one launch (start us, length us, event | category | flops | bytes accessed | tf_op | source)
XLA Modules:
  0.0 478.3 jit_solution(2086190551319542798)
XLA Ops:
  51.3 4.5 fusion.50
  63.6 17.9 %fusion.58 = f32[1,2,4,16,16,128]{5,4,3,2,1,0:T(8,128)S(1)} fusion(f32[1,2,4,16,24,4]{5,4,3,2,1,0:T(8,128)} %copy.96, f32[1,2,4,16,24,128]{5,4,3,2,1,0:T(8,128)} %copy.93, f32[1,2,4,16,24,4]{5,4,3,2,1,0:T(8,128)} %copy.94, f32[1,2,4,15,16,128]{5,4,3,2,1,0:T(8,128)} %copy.87, f32[1,2,4,1,16,128]{5,4,3,2,1,0:T(8,128)} %bitcast.76, ...), kind=kLoop, calls=%fused_computation.166 | loop fusion | flops 12845056 | bytes 20676608 | tf_op jit(solution)/shard_map/add | solution.py:51
  83.0 6.7 %all-reduce.2 = (f32[4]{0:T(128)S(1)}, f32[4]{0:T(128)S(1)}, f32[4]{0:T(128)S(1)}, f32[4]{0:T(128)S(1)}) all-reduce(f32[4]{0:T(128)S(1)} %get-tuple-element.10, f32[4]{0:T(128)S(1)} %get-tuple-element.9, f32[4]{0:T(128)S(1)} %get-tuple-element.12, f32[4]{0:T(128)S(1)} %get-tuple-element.11), channel_id=1, replica_groups=mesh['quad'=2,'py'=4,'pz'=4] {'py'}, use_global_device_ids=true, to_apply=%region_10.11 | all-reduce | flops 16 | bytes 128 | tf_op jit(solution)/shard_map/psum | solution.py:13
  89.7 12.9 %all-reduce.1 = (f32[4]{0:T(128)S(1)}, f32[4]{0:T(128)S(1)}, f32[4]{0:T(128)S(1)}, f32[4]{0:T(128)S(1)}) all-reduce(f32[4]{0:T(128)S(1)} %get-tuple-element.21, f32[4]{0:T(128)S(1)} %get-tuple-element.22, f32[4]{0:T(128)S(1)} %get-tuple-element.23, f32[4]{0:T(128)S(1)} %get-tuple-element.24), channel_id=1, replica_groups=mesh['quad'=2,'py'=4,'pz'=4] {'pz'}, use_global_device_ids=true, to_apply=%region_11.12 | all-reduce | flops 16 | bytes 128 | tf_op jit(solution)/shard_map/psum | solution.py:14
  109.4 3.5 fusion.31
  118.6 19.1 %copy.121 = f32[4,2,4,16,16,128]{4,3,5,2,1,0:T(8,128)} copy(f32[4,2,4,16,16,128]{5,4,3,2,1,0:T(8,128)} %pad_maximum_fusion.1) | data formatting | bytes 8388608 | tf_op jit(solution)/shard_map/stack | solution.py:119
  147.0 3.4 fusion.25
  150.4 18.9 %copy.122 = f32[4,2,4,16,4,128]{4,3,5,2,1,0:T(8,128)} copy(f32[4,2,4,16,4,128]{5,3,4,2,1,0:T(8,128)} %collective-permute-done.4) | data formatting | bytes 2097152 | tf_op jit(solution)/shard_map/ppermute | solution.py:26
  169.3 18.6 %copy.120 = f32[4,2,4,16,4,128]{4,3,5,2,1,0:T(8,128)} copy(f32[4,2,4,16,4,128]{5,3,4,2,1,0:T(8,128)} %collective-permute-done.5) | data formatting | bytes 2097152 | tf_op jit(solution)/shard_map/ppermute | solution.py:23
  187.9 43.9 %pad_maximum_fusion = f32[4,2,4,16,24,128]{4,3,5,2,1,0:T(8,128)} fusion(f32[4,2,4,16,4,128]{4,3,5,2,1,0:T(8,128)} %copy.122, f32[4,2,4,16,16,128]{4,3,5,2,1,0:T(8,128)} %copy.121, f32[4,2,4,16,4,128]{4,3,5,2,1,0:T(8,128)} %copy.120), kind=kLoop, calls=%fused_computation | loop fusion | flops 3145728 | bytes 12582912 | tf_op jit(solution)/shard_map/concatenate | solution.py:27
  234.9 4.0 collective-permute-start.6
  242.2 5.5 %pad_maximum_fusion.2 = (f32[4,2,4,16,20,128]{5,4,3,2,1,0:T(8,128)}, f32[4,2,4,16,20,128]{5,4,3,2,1,0:T(8,128)}) fusion(f32[4,2,4,16,4,128]{5,4,3,2,1,0:T(4,128)S(1)} %copy.117, f32[4,1,4,16,16,128]{5,4,3,2,1,0:T(8,128)S(1)} %get-tuple-element.52, f32[4,1,4,16,16,128]{5,4,3,2,1,0:T(8,128)S(1)} %copy-done.2, f32[4,2,4,16,4,128]{5,4,3,2,1,0:T(4,128)S(1)} %copy.119), kind=kLoop, calls=%fused_computation.50 | loop fusion | flops 5242880 | bytes 16777216 | tf_op jit(solution)/shard_map/concatenate | solution.py:27
  247.7 22.1 %copy.123 = f32[4,2,4,16,24,128]{5,4,3,2,1,0:T(8,128)} copy(f32[4,2,4,16,24,128]{4,3,5,2,1,0:T(8,128)} %pad_maximum_fusion) | data formatting | bytes 12582912 | tf_op jit(solution)/shard_map/concatenate | solution.py:27
  269.7 6.1 %copy.125 = f32[4,2,4,16,24,4]{5,4,3,2,1,0:T(8,128)} copy(f32[4,2,4,16,24,4]{4,3,5,2,1,0:T(8,128)} %collective-permute-done.7) | data formatting | bytes 393216 | tf_op jit(solution)/shard_map/ppermute | solution.py:23
  275.8 7.1 %collective-permute-done.6 = f32[4,2,4,16,24,4]{4,3,5,2,1,0:T(8,128)} collective-permute-done((f32[4,2,4,16,24,4]{4,3,5,2,1,0:T(8,128)}, f32[4,2,4,16,24,4]{4,3,5,2,1,0:T(8,128)}, u32[]{:S(2)}, u32[]{:S(2)}) %collective-permute-start.6) | collective-permute-done | bytes 196640 | tf_op jit(solution)/shard_map/ppermute | solution.py:26
  282.9 6.0 %copy.124 = f32[4,2,4,16,24,4]{5,4,3,2,1,0:T(8,128)} copy(f32[4,2,4,16,24,4]{4,3,5,2,1,0:T(8,128)} %collective-permute-done.6) | data formatting | bytes 393216 | tf_op jit(solution)/shard_map/ppermute | solution.py:26
  289.0 63.1 %fusion.6 = f32[4,2,4,16,16,128]{5,4,3,2,1,0:T(8,128)} fusion(f32[4,2,4,16,24,4]{5,4,3,2,1,0:T(8,128)} %copy.125, f32[4,2,4,16,24,128]{5,4,3,2,1,0:T(8,128)} %copy.123, f32[4,2,4,16,24,4]{5,4,3,2,1,0:T(8,128)} %copy.124, f32[4,2,4,16,20,128]{5,4,3,2,1,0:T(8,128)} %get-tuple-element.47, f32[4,2,4,16,20,128]{5,4,3,2,1,0:T(8,128)} %get-tuple-element.46, ...), kind=kLoop, calls=%fused_computation.70 | loop fusion | flops 51380224 | bytes 82313216 | tf_op jit(solution)/shard_map/add | solution.py:51
  352.1 5.0 %subtract_reduce_fusion = (f32[4,4]{1,0:T(4,128)S(1)}, f32[4,4]{1,0:T(4,128)S(1)}, f32[4,4]{1,0:T(4,128)S(1)}, f32[4,4]{1,0:T(4,128)S(1)}) fusion(f32[4,2,4,16,16,128]{5,4,3,2,1,0:T(8,128)} %fusion.6, f32[4]{0:T(128)S(1)} %get-tuple-element.92, f32[4]{0:T(128)S(1)} %get-tuple-element.93, f32[4,16,16,128]{3,2,1,0:T(8,128)S(1)} %copy-done.8, ...), kind=kLoop, calls=%fused_computation.129 | loop fusion | flops 20447168 | bytes 6291872 | tf_op jit(solution)/shard_map/reduce_sum | solution.py:68
  357.1 32.4 %all-reduce = (f32[4,4]{1,0:T(4,128)S(1)}, f32[4,4]{1,0:T(4,128)S(1)}, f32[4,4]{1,0:T(4,128)S(1)}, f32[4,4]{1,0:T(4,128)S(1)}) all-reduce(f32[4,4]{1,0:T(4,128)S(1)} %get-tuple-element.8, f32[4,4]{1,0:T(4,128)S(1)} %get-tuple-element.6, f32[4,4]{1,0:T(4,128)S(1)} %get-tuple-element.7, ...), channel_id=1, replica_groups=mesh['quad'=2,'py'=4,'pz'=4] {'py','pz'}, use_global_device_ids=true, to_apply=%region_13.14 | all-reduce | flops 64 | bytes 512 | tf_op jit(solution)/shard_map/psum | solution.py:124
  392.6 4.4 fusion.34
  397.0 4.4 fusion.36
  401.4 4.6 add_bitcast_fusion
  406.0 4.9 %subtract_bitcast_fusion = f32[4,1,4,16,16,128]{5,0,4,3,2,1:T(4,128)S(1)} fusion(f32[4,4,16,16,128]{4,0,3,2,1:T(4,128)S(1)} %fusion.36, f32[4,4,16,16,128]{4,3,2,1,0:T(8,128)S(1)} %get-tuple-element.50, f32[4]{0:T(128)S(1)} %copy-done.20, f32[4]{0:T(128)S(1)} %copy-done.21, f32[]{:T(128)S(6)} %div.49), kind=kOutput, calls=%fused_computation.123 | convolution fusion | flops 25690144 | bytes 6291492 | tf_op jit(solution)/shard_map/kq,qsxyz->ksxyz/dot_general | solution.py:81
  415.6 52.3 %reduce-scatter.2.cloned.1.call-done = f32[4,2,4,8,16,128]{5,4,2,1,0,3:T(8,128)} async-done(((f32[4,2,4,16,16,128]{5,4,2,1,0,3:T(8,128)}), f32[4,2,4,8,16,128]{5,4,2,1,0,3:T(8,128)}) %reduce-scatter.2.cloned.1.call-update) | async-done | bytes 2097168 | tf_op jit(solution)/shard_map/reduce_scatter | solution.py:136
  (137 shorter events, 91.7 us)
Async XLA Ops:
  6.5 461.4 %reduce-scatter.2.cloned.1.call-start = ((), (), s32[]{:S(2)}) async-start(), calls=%async_computation.1 | async-start | bytes 6291456 | tf_op jit(solution)/shard_map/reduce_scatter | solution.py:136
  9.0 28.6 %collective-permute-start = (f32[1,2,4,16,4,128]{5,3,4,2,1,0:T(8,128)}, f32[1,2,4,16,4,128]{5,3,4,2,1,0:T(8,128)}, u32[]{:S(2)}, u32[]{:S(2)}) collective-permute-start(f32[1,2,4,16,4,128]{5,3,4,2,1,0:T(8,128)} %get-tuple-element.87), channel_id=1, source_target_pairs={{4,0},{8,4},{12,8},{0,12},{5,1},{9,5},{13,9},{1,13},{6,2},{10,6},{... | collective-permute-start | bytes 786440 | tf_op jit(solution)/shard_map/ppermute | solution.py:26
  11.4 26.2 %collective-permute-start.1 = (f32[1,2,4,16,4,128]{5,3,4,2,1,0:T(8,128)}, f32[1,2,4,16,4,128]{5,3,4,2,1,0:T(8,128)}, u32[]{:S(2)}, u32[]{:S(2)}) collective-permute-start(f32[1,2,4,16,4,128]{5,3,4,2,1,0:T(8,128)} %get-tuple-element.86), channel_id=1, source_target_pairs={{0,4},{4,8},{8,12},{12,0},{1,5},{5,9},{9,13},{13,1},{2,6},{6,10},{... | collective-permute-start | bytes 786440 | tf_op jit(solution)/shard_map/ppermute | solution.py:23
  44.0 13.5 %collective-permute-start.3 = (f32[1,2,4,16,24,4]{4,3,5,2,1,0:T(8,128)}, f32[1,2,4,16,24,4]{4,3,5,2,1,0:T(8,128)}, u32[]{:S(2)}, u32[]{:S(2)}) collective-permute-start(f32[1,2,4,16,24,4]{4,3,5,2,1,0:T(8,128)} %copy.95), channel_id=1, source_target_pairs={{0,1},{1,2},{2,3},{3,0},{4,5},{5,6},{6,7},{7,4},{8,9},{9,10},{10,1... | collective-permute-start | bytes 147464 | tf_op jit(solution)/shard_map/ppermute | solution.py:23
  48.5 12.1 %collective-permute-start.2 = (f32[1,2,4,16,24,4]{4,3,5,2,1,0:T(8,128)}, f32[1,2,4,16,24,4]{4,3,5,2,1,0:T(8,128)}, u32[]{:S(2)}, u32[]{:S(2)}) collective-permute-start(f32[1,2,4,16,24,4]{4,3,5,2,1,0:T(8,128)} %copy.92), channel_id=1, source_target_pairs={{1,0},{2,1},{3,2},{0,3},{5,4},{6,5},{7,6},{4,7},{9,8},{10,9},{11,1... | collective-permute-start | bytes 147464 | tf_op jit(solution)/shard_map/ppermute | solution.py:26
  55.8 7.8 %copy-start.3 = (f32[4,16,16,128]{3,2,1,0:T(8,128)S(1)}, f32[4,16,16,128]{3,2,1,0:T(8,128)}, u32[]{:S(2)}) copy-start(f32[4,16,16,128]{3,2,1,0:T(8,128)} %param.6) | copy-start | bytes 1572868
  55.8 7.8 %copy-start.4 = (f32[4,16,16,128]{3,2,1,0:T(8,128)S(1)}, f32[4,16,16,128]{3,2,1,0:T(8,128)}, u32[]{:S(2)}) copy-start(f32[4,16,16,128]{3,2,1,0:T(8,128)} %param.5) | copy-start | bytes 1572868
  81.4 21.3 %copy-start.5 = (f32[4,16,16,128]{3,2,1,0:T(8,128)S(1)}, f32[4,16,16,128]{3,2,1,0:T(8,128)}, u32[]{:S(2)}) copy-start(f32[4,16,16,128]{3,2,1,0:T(8,128)} %param.5) | copy-start | bytes 1572868
  102.6 11.9 %copy-start.26 = (f32[4]{0:T(128)}, f32[4]{0:T(128)S(1)}, u32[]{:S(2)}) copy-start(f32[4]{0:T(128)S(1)} %get-tuple-element.19) | copy-start | bytes 52
  102.6 11.8 %copy-start.28 = (f32[4]{0:T(128)}, f32[4]{0:T(128)S(1)}, u32[]{:S(2)}) copy-start(f32[4]{0:T(128)S(1)} %get-tuple-element.20) | copy-start | bytes 52
  105.2 12.7 %copy-start = (f32[4,1,4,16,16,128]{5,4,3,2,1,0:T(8,128)}, f32[4,1,4,16,16,128]{5,4,3,2,1,0:T(8,128)S(1)}, u32[]{:S(2)}) copy-start(f32[4,1,4,16,16,128]{5,4,3,2,1,0:T(8,128)S(1)} %get-tuple-element.53) | copy-start | bytes 6291460
  116.1 34.3 %collective-permute-start.4 = (f32[4,2,4,16,4,128]{5,3,4,2,1,0:T(8,128)}, f32[4,2,4,16,4,128]{5,3,4,2,1,0:T(8,128)}, u32[]{:S(2)}, u32[]{:S(2)}) collective-permute-start(f32[4,2,4,16,4,128]{5,3,4,2,1,0:T(8,128)} %copy.144), channel_id=1, source_target_pairs={{4,0},{8,4},{12,8},{0,12},{5,1},{9,5},{13,9},{1,13},{6,2},{10,6},{... | collective-permute-start | bytes 3145736 | tf_op jit(solution)/shard_map/ppermute | solution.py:26
  117.2 52.1 %collective-permute-start.5 = (f32[4,2,4,16,4,128]{5,3,4,2,1,0:T(8,128)}, f32[4,2,4,16,4,128]{5,3,4,2,1,0:T(8,128)}, u32[]{:S(2)}, u32[]{:S(2)}) collective-permute-start(f32[4,2,4,16,4,128]{5,3,4,2,1,0:T(8,128)} %copy.145), channel_id=1, source_target_pairs={{0,4},{4,8},{8,12},{12,0},{1,5},{5,9},{9,13},{13,1},{2,6},{6,10},{... | collective-permute-start | bytes 3145736 | tf_op jit(solution)/shard_map/ppermute | solution.py:23
  234.9 34.9 %collective-permute-start.7 = (f32[4,2,4,16,24,4]{4,3,5,2,1,0:T(8,128)}, f32[4,2,4,16,24,4]{4,3,5,2,1,0:T(8,128)}, u32[]{:S(2)}, u32[]{:S(2)}) collective-permute-start(f32[4,2,4,16,24,4]{4,3,5,2,1,0:T(8,128)} %get-tuple-element.29), channel_id=1, source_target_pairs={{0,1},{1,2},{2,3},{3,0},{4,5},{5,6},{6,7},{7,4},{8,9},{9,10},{10,1... | collective-permute-start | bytes 589832 | tf_op jit(solution)/shard_map/ppermute | solution.py:23
  234.9 48.1 %collective-permute-start.6 = (f32[4,2,4,16,24,4]{4,3,5,2,1,0:T(8,128)}, f32[4,2,4,16,24,4]{4,3,5,2,1,0:T(8,128)}, u32[]{:S(2)}, u32[]{:S(2)}) collective-permute-start(f32[4,2,4,16,24,4]{4,3,5,2,1,0:T(8,128)} %get-tuple-element.28), channel_id=1, source_target_pairs={{1,0},{2,1},{3,2},{0,3},{5,4},{6,5},{7,6},{4,7},{9,8},{10,9},{11,1... | collective-permute-start | bytes 589832 | tf_op jit(solution)/shard_map/ppermute | solution.py:26
  289.0 63.1 %copy-start.6 = (f32[4,16,16,128]{3,2,1,0:T(8,128)S(1)}, f32[4,16,16,128]{3,2,1,0:T(8,128)}, u32[]{:S(2)}) copy-start(f32[4,16,16,128]{3,2,1,0:T(8,128)} %get-tuple-element.64) | copy-start | bytes 1572868
  289.0 63.1 %copy-start.8 = (f32[4,16,16,128]{3,2,1,0:T(8,128)S(1)}, f32[4,16,16,128]{3,2,1,0:T(8,128)}, u32[]{:S(2)}) copy-start(f32[4,16,16,128]{3,2,1,0:T(8,128)} %get-tuple-element.65) | copy-start | bytes 1572868
  352.1 37.4 %copy-start.23 = (f32[4]{0:T(128)S(1)}, f32[4]{0:T(128)}, u32[]{:S(2)}) copy-start(f32[4]{0:T(128)} %copy-done.22) | copy-start | bytes 52
  352.1 37.4 %copy-start.25 = (f32[4]{0:T(128)S(1)}, f32[4]{0:T(128)}, u32[]{:S(2)}) copy-start(f32[4]{0:T(128)} %copy-done.24) | copy-start | bytes 52
  352.1 37.4 %copy-start.27 = (f32[4]{0:T(128)S(1)}, f32[4]{0:T(128)}, u32[]{:S(2)}) copy-start(f32[4]{0:T(128)} %copy-done.26) | copy-start | bytes 52
  352.1 37.4 %copy-start.29 = (f32[4]{0:T(128)S(1)}, f32[4]{0:T(128)}, u32[]{:S(2)}) copy-start(f32[4]{0:T(128)} %copy-done.28) | copy-start | bytes 52
  352.1 37.4 %copy-start.30 = (f32[4]{0:T(128)S(1)}, f32[4]{0:T(128)}, u32[]{:S(2)}) copy-start(f32[4]{0:T(128)} %multiply_add_fusion.4) | copy-start | bytes 52
  352.1 37.6 %copy-start.7 = (f32[4,16,16,128]{3,2,1,0:T(8,128)S(1)}, f32[4,16,16,128]{3,2,1,0:T(8,128)}, u32[]{:S(2)}) copy-start(f32[4,16,16,128]{3,2,1,0:T(8,128)} %get-tuple-element.64) | copy-start | bytes 1572868
  352.1 37.6 %copy-start.9 = (f32[4,16,16,128]{3,2,1,0:T(8,128)S(1)}, f32[4,16,16,128]{3,2,1,0:T(8,128)}, u32[]{:S(2)}) copy-start(f32[4,16,16,128]{3,2,1,0:T(8,128)} %get-tuple-element.65) | copy-start | bytes 1572868
  (16 other events, 82.4 us)
Sparse Core Ops, SparseCore 0:
  415.8 52.1 reduce-scatter.1
